TPU v7x, 128 devices: a whole 4x4x4 slice. The times are simulated.
128 devices in a mesh: ka: 64 (over y, z, x_lo, core), pa: 2 (over x_hi).
Axes of the slice: x: 4 (x_hi: 2, x_lo: 2; x = x_hi * 2 + x_lo), y: 4, z: 4, core: 2. Of those that a mesh axis runs over, the one named last changes fastest.
Arguments:
- conduction: bfloat16 [64, 48, 2048], P('ka'), may hold values from -6 to 6
- weighted: bfloat16 [64, 48, 2048], P('ka'), may hold values from -6 to 6
- valence: bfloat16 [64, 64, 2048], P('ka', None, 'pa'), may hold values from -0.015625 to 0.015625
- screening: bfloat16 [64, 2048, 2048], P('ka', None, 'pa'), may hold values from -0.125 to 0.125
- pair_transfer: int32 [64, 64], replicated, may hold values from 0 to 63, as said below
- owner_map: int32 [64], replicated, may hold values from 0 to 63, each once
Outputs:
- kernel_out: float32 [64, 48, 64], P('ka')
Inputs may be any that keep to these rules, and one draw needn't show every extreme that they name: pair_transfer[i, j] = (g_i - g_j) mod 64 for positions g of the k-points on a cyclic grid of 64 points (a permutation drawn from the seed), so each row and each column names every transfer once. `owner_map`: each transfer is held by exactly one slot.
All inputs are finite; a program needn't handle non-finite values.
Results may differ from a plain program's by a relative error of at most 0.0029.
Values may be sent and summed in bfloat16 or wider, within the bound.
No kernel may reach another device: no remote copies, remote signals or barrier semaphores. Data moves between devices by JAX's collectives and lax.ppermute only.
A program may use at most 128 MiB of HBM per device.

v0:
```python
import jax
import jax.numpy as jnp
from jax import lax
from jax.sharding import PartitionSpec as P


def in_blocks(x, dim, peers):
    before, after = (x.shape[:dim], x.shape[dim + 1 :])
    return jnp.moveaxis(x.reshape(*before, peers, -1, *after), dim, 0)


def sent_and_summed(x, axis, dim):
    peers = lax.axis_size(axis)
    blocks = lax.all_to_all(in_blocks(x, dim, peers), axis, 0, 0, tiled=True)
    return jnp.sum(blocks, axis=0)


def over_pieces(x, axis):
    return lax.all_gather(x, axis).sum(0)


def shards(conduction, weighted, valence, screening, pair_transfer, owner_map):
    local_count = conduction.shape[0]
    half_width = screening.shape[2]
    first_column = lax.axis_index("pa") * half_width
    first_slot = lax.axis_index("ka") * local_count
    owned_transfers = lax.dynamic_slice_in_dim(owner_map, first_slot, local_count)
    columns = jnp.arange(pair_transfer.shape[1], dtype=jnp.int32)
    matches = pair_transfer[None, :, :] == owned_transfers[:, None, None]
    partners = jnp.sum(jnp.where(matches, columns[None, None, :], 0), axis=2)
    every_cond = lax.all_gather(conduction, "ka", axis=0, tiled=True)
    piece = lax.all_gather(weighted, "ka", axis=0, tiled=True)
    count = piece.shape[0]
    total = jnp.zeros((count, piece.shape[1], half_width), jnp.float32)
    partner_rows = partners[0]
    partner_cond = jnp.take(every_cond, partner_rows, axis=0)
    density = (partner_cond.astype(jnp.float32) * piece.astype(jnp.float32)).astype(jnp.bfloat16)
    screened = jnp.dot(
        density.reshape(-1, density.shape[2]), screening[0], preferred_element_type=jnp.float32
    )
    partner_half = lax.dynamic_slice_in_dim(partner_cond, first_column, half_width, 2)
    total = partner_half.astype(jnp.float32) * screened.reshape(total.shape)
    every_valence = lax.all_gather(valence, "ka", axis=0, tiled=True)
    owner_terms = jnp.einsum(
        "kbp,kvp->kbv", total, every_valence.astype(jnp.float32), precision=lax.Precision.HIGHEST
    )
    partial_out = sent_and_summed(owner_terms, "ka", 0)
    return over_pieces(partial_out, "pa")


def solution(mesh):
    in_specs = (
        P("ka", None, None),
        P("ka", None, None),
        P("ka", None, "pa"),
        P("ka", None, "pa"),
        P(),
        P(),
    )
    out_specs = P("ka", None, None)
    return jax.shard_map(shards, mesh=mesh, in_specs=in_specs, out_specs=out_specs, check_vma=False)
```

profile of v0, /device:TPU:0, one launch (start us, length us, event | category | flops | bytes accessed | tf_op | source)
XLA Modules:
  0.0 408.6 jit_solution(18051606673469656491)
XLA Ops:
  6.5 0.0 all-gather.5.cloned.1.call-start
  6.5 0.7 all-gather.5.cloned.1.call-update
  7.3 0.0 all-gather.7.cloned.1.call-start
  7.3 0.7 all-gather.7.cloned.1.call-update
  8.0 0.0 all-gather.9.cloned.1.call-start
  8.1 0.7 all-gather.9.cloned.1.call-update
  8.7 1.2 dynamic_slice.6
  10.0 1.5 select_reduce_fusion
  11.5 116.5 %all-gather.5.cloned.1.call-done = bf16[64,48,2048]{2,1,0:T(8,128)(2,1)} async-done(((bf16[1,48,2048]{2,1,0:T(8,128)(2,1)}), bf16[64,48,2048]{2,1,0:T(8,128)(2,1)}) %all-gather.5.cloned.1.call-update) | async-done | bytes 12582928 | tf_op jit(solution)/shard_map/all_gather | solution.py:31
  128.1 12.1 %gather_fusion = bf16[64,48,2048]{2,1,0:T(8,128)(2,1)} fusion(bf16[64,48,2048]{2,1,0:T(8,128)(2,1)} %all-gather.5.cloned.1.call-done, s32[1024]{0:T(1024)S(1)} %pad_clamp_fusion), kind=kCustom, calls=%fused_computation | custom fusion | bytes 25166080 | tf_op jit(solution)/shard_map/jit(_take)/gather | solution.py:36
  140.1 10.9 %broadcast_select_fusion = bf16[64,48,2048]{2,1,0:T(8,128)(2,1)} fusion(bf16[64,48,2048]{2,1,0:T(8,128)(2,1)} %gather_fusion, pred[64]{0:T(512)(128)(4,1)S(1)} %compare_and_fusion), kind=kLoop, calls=%fused_computation.6 | loop fusion | flops 6291456 | bytes 25165888 | tf_op jit(solution)/shard_map/jit(_take)/select_n | solution.py:36
  151.0 94.0 %all-gather.7.cloned.1.call-done = bf16[64,48,2048]{2,1,0:T(8,128)(2,1)} async-done(((bf16[1,48,2048]{2,1,0:T(8,128)(2,1)}), bf16[64,48,2048]{2,1,0:T(8,128)(2,1)}) %all-gather.7.cloned.1.call-update) | async-done | bytes 12582928 | tf_op jit(solution)/shard_map/all_gather | solution.py:32
  245.0 21.8 %fusion = f32[64,48,1024]{2,1,0:T(8,128)} fusion(bf16[64,48,2048]{2,1,0:T(8,128)(2,1)} %all-gather.7.cloned.1.call-done, bf16[64,48,2048]{2,1,0:T(8,128)(2,1)} %broadcast_select_fusion, bf16[1,2048,1024]{2,1,0:T(8,128)(2,1)} %param.9), kind=kOutput, calls=%fused_computation.2 | convolution fusion | flops 12910067712 | bytes 41943040 | tf_op jit(solution)/shard_map/dot_general | solution.py:38
  266.9 89.3 %all-gather.9.cloned.1.call-done = bf16[64,64,1024]{2,1,0:T(8,128)(2,1)} async-done(((bf16[1,64,1024]{2,1,0:T(8,128)(2,1)}), bf16[64,64,1024]{2,1,0:T(8,128)(2,1)}) %all-gather.9.cloned.1.call-update) | async-done | bytes 8388624 | tf_op jit(solution)/shard_map/all_gather | solution.py:43
  356.2 13.1 %fusion.6 = f32[64,1,48,64]{3,2,1,0:T(8,128)S(1)} fusion(bf16[64,64,1024]{2,1,0:T(8,128)(2,1)} %all-gather.9.cloned.1.call-done, f32[64,48,1024]{2,1,0:T(8,128)} %fusion, bf16[64,48,2048]{2,1,0:T(8,128)(2,1)} %broadcast_select_fusion, s32[]{:T(128)S(6)} %select_n.36), kind=kOutput, calls=%fused_computation.9 | convolution fusion | flops 2422210560 | bytes 28049412 | tf_op jit(solution)/shard_map/kbp,kvp->kbv/dot_general | solution.py:44
  369.3 1.0 reshape.50
  370.3 21.6 %all_to_all.5 = f32[64,1,3072]{2,1,0:T(1,128)S(1)} all-to-all(f32[64,1,3072]{2,1,0:T(1,128)S(1)} %reshape.50), channel_id=1, replica_groups=mesh['ka'=64,'pa'=2] {'ka'}, dimensions={0} | all-to-all | bytes 1572864 | tf_op jit(solution)/shard_map/all_to_all | solution.py:14
  391.9 0.5 broadcast.33
  392.4 2.5 reduce.5
  394.9 0.4 reshape.51
  395.3 0.1 reduce_sum.33
  395.5 6.0 %all-gather = f32[96,64]{1,0:T(8,128)S(1)} all-gather(f32[48,64]{1,0:T(8,128)S(1)} %reduce_sum.33), channel_id=2, replica_groups=mesh['ka'=64,'pa'=2] {'pa'}, dimensions={0}, use_global_device_ids=true | all-gather | bytes 36864 | tf_op jit(solution)/shard_map/all_gather | solution.py:19
  401.5 0.6 reduce.4
  (3 shorter events, 0.0 us)
Async XLA Ops:
  6.5 121.5 %all-gather.5.cloned.1.call-start = ((), (), s32[]{:S(2)}) async-start(), calls=%async_computation.1 | async-start | bytes 12779520 | tf_op jit(solution)/shard_map/all_gather | solution.py:31
  7.3 237.8 %all-gather.7.cloned.1.call-start = ((), (), s32[]{:S(2)}) async-start(), calls=%async_computation.2 | async-start | bytes 12779520 | tf_op jit(solution)/shard_map/all_gather | solution.py:32
  8.0 348.2 %all-gather.9.cloned.1.call-start = ((), (), s32[]{:S(2)}) async-start(), calls=%async_computation.3 | async-start | bytes 8519680 | tf_op jit(solution)/shard_map/all_gather | solution.py:43
Sparse Core Ops, SparseCore 0:
  9.0 118.9 all-gather.4
  129.8 115.2 all-gather.6
  246.8 109.4 all-gather.8
where the time goes:
time: 409 us
  waiting for transfers between devices  302 us (74%)
  matrix products  34.9 us (9%)
  blocking collectives  27.6 us (7%)
  other arithmetic  15.7 us (4%)
  local copies, waits for them, and re-layouts  15.2 us (4%)
  between operations  13.2 us (3%)
    all_gather x1, waiting for transfers between devices, shards(): every_cond = lax.all_gather(conduction, 'ka', axis=0, tiled=True)  117 us
    all_gather x1, waiting for transfers between devices, shards(): piece = lax.all_gather(weighted, 'ka', axis=0, tiled=True)  94 us
    all_gather x1, waiting for transfers between devices, shards(): every_valence = lax.all_gather(valence, 'ka', axis=0, tiled=True)  89.3 us
    dot_general x1, matrix products, shards(): jnp.dot(density.reshape(-1, density.shape[2]), screening[0], preferred_el...  21.8 us
    all_to_all x1, blocking collectives, sent_and_summed(): blocks = lax.all_to_all(in_blocks(x, dim, peers), axis, 0, 0, tiled=True)  21.6 us
    dot_general x1, matrix products, shards(): jnp.einsum('kbp,kvp->kbv', total, every_valence.astype(jnp.float32), prec...  13.1 us
    gather x1, local copies, waits for them, and re-layouts, shards(): partner_cond = jnp.take(every_cond, partner_rows, axis=0)  12.1 us
    select_n x2, other arithmetic, shards(): partner_cond = jnp.take(every_cond, partner_rows, axis=0)  10.9 us
  transfers between devices with their start and end apart: 3, of which 3 were waited for; matrix products, arithmetic and copies ran while one was open for 12% of the time, Pallas kernels for 0%

commit v1 on v0

--- a/solution.py
+++ b/solution.py
@@ -29,7 +29,9 @@
     matches = pair_transfer[None, :, :] == owned_transfers[:, None, None]
     partners = jnp.sum(jnp.where(matches, columns[None, None, :], 0), axis=2)
     every_cond = lax.all_gather(conduction, "ka", axis=0, tiled=True)
-    piece = lax.all_gather(weighted, "ka", axis=0, tiled=True)
+    piece = jnp.concatenate(
+        lax.all_to_all(jnp.stack([weighted] * lax.axis_size("ka")), "ka", 0, 0), axis=0
+    )
     count = piece.shape[0]
     total = jnp.zeros((count, piece.shape[1], half_width), jnp.float32)
     partner_rows = partners[0]

time: 409 us -> 441 us (1.078)
  waiting for transfers between devices: 302 us -> 328 us
  other arithmetic: 15.7 us -> 4.03 us
  starting transfers between devices: 0.08 us -> 10.4 us
  local copies, waits for them, and re-layouts: 15.2 us -> 21.4 us
    all_gather x1, waiting for transfers between devices: 117 us -> 248 us  [shards(): every_cond = lax.all_gather(conduction, 'ka', axis=0, tiled=True)]
    all_gather x1 -> x0, waiting for transfers between devices: 94 us -> none  [shards(): piece = lax.all_gather(weighted, 'ka', axis=0, tiled=True)]
    select_n x2 -> x1, other arithmetic: 10.9 us -> 0.01 us  [shards(): partner_cond = jnp.take(every_cond, partner_rows, axis=0)]
    all_gather x1, waiting for transfers between devices: 89.3 us -> 78.6 us  [shards(): every_valence = lax.all_gather(valence, 'ka', axis=0, tiled=True)]
    all_to_all x0 -> x1, starting transfers between devices: none -> 10.4 us  [shards(): lax.all_to_all(jnp.stack([weighted] * lax.axis_size('ka')), 'ka', 0, 0)]
    another operation x0 -> x1, local copies, waits for them, and re-layouts: none -> 6.97 us  [shards(): jnp.stack([weighted] * lax.axis_size('ka'))]
  transfers between devices with their start and end apart: 3 -> 3, of which waited for: 3 -> 2; matrix products, arithmetic and copies ran while one was open for 12% -> 10% of each run, Pallas kernels for 0% -> 0%
where the time goes in v1:
time: 441 us; the launch traced here: 440 us
  waiting for transfers between devices  328 us (74%)
  matrix products  35.7 us (8%)
  blocking collectives  27.3 us (6%)
  local copies, waits for them, and re-layouts  21.4 us (5%)
  between operations  13.5 us (3%)
  starting transfers between devices  10.4 us (2%)
    all_gather x1, waiting for transfers between devices, shards(): every_cond = lax.all_gather(conduction, 'ka', axis=0, tiled=True)  248 us
    all_gather x1, waiting for transfers between devices, shards(): every_valence = lax.all_gather(valence, 'ka', axis=0, tiled=True)  78.6 us
    dot_general x1, matrix products, shards(): jnp.dot(density.reshape(-1, density.shape[2]), screening[0], preferred_el...  22.1 us
    all_to_all x1, blocking collectives, sent_and_summed(): blocks = lax.all_to_all(in_blocks(x, dim, peers), axis, 0, 0, tiled=True)  21.3 us
    dot_general x1, matrix products, shards(): jnp.einsum('kbp,kvp->kbv', total, every_valence.astype(jnp.float32), prec...  13.6 us
    gather x1, local copies, waits for them, and re-layouts, shards(): partner_cond = jnp.take(every_cond, partner_rows, axis=0)  11.9 us
    all_to_all x1, starting transfers between devices, shards(): lax.all_to_all(jnp.stack([weighted] * lax.axis_size('ka')), 'ka', 0, 0)  10.4 us
  transfers between devices with their start and end apart: 3, of which 2 were waited for; matrix products, arithmetic and copies ran while one was open for 10% of the time, Pallas kernels for 0%

profile of v1, /device:TPU:0, one launch (start us, length us, event | category | flops | bytes accessed | tf_op | source)
XLA Modules:
  0.0 440.3 jit_solution(4870692163867513016)
XLA Ops:
  6.5 0.0 all-gather.4.cloned.1.call-start
  6.5 0.7 all-gather.4.cloned.1.call-update
  7.3 7.0 %stack.2 = bf16[64,1,48,2048]{3,2,1,0:T(8,128)(2,1)} broadcast(bf16[48,2048]{1,0:T(8,128)(2,1)} %bitcast.31), dimensions={2,3} | broadcast | bytes 12779520 | tf_op jit(solution)/shard_map/stack | solution.py:33
  14.2 10.4 %all-to-all-start = ((bf16[64,1,48,2048]{3,2,1,0:T(8,128)(2,1)}), bf16[64,1,48,2048]{3,2,1,0:T(8,128)(2,1)}, u32[]{:S(2)}, u32[]{:S(2)}) async-start(bf16[64,1,48,2048]{3,2,1,0:T(8,128)(2,1)} %stack.2), calls=%async_computation | async-start | bytes 25165824 | tf_op jit(solution)/shard_map/all_to_all | solution.py:33
  24.6 0.0 all-gather.6.cloned.1.call-start
  24.6 0.7 all-gather.6.cloned.1.call-update
  25.4 0.0 copy-done.1
  25.4 0.6 dynamic_slice.6
  26.0 0.0 copy-done
  26.0 0.7 select_reduce_fusion
  26.7 248.0 %all-gather.4.cloned.1.call-done = bf16[64,48,2048]{2,1,0:T(8,128)(2,1)} async-done(((bf16[1,48,2048]{2,1,0:T(8,128)(2,1)}), bf16[64,48,2048]{2,1,0:T(8,128)(2,1)}) %all-gather.4.cloned.1.call-update) | async-done | bytes 12582928 | tf_op jit(solution)/shard_map/all_gather | solution.py:31
  274.8 11.9 %gather_fusion = bf16[64,48,2048]{2,1,0:T(8,128)(2,1)} fusion(bf16[64,48,2048]{2,1,0:T(8,128)(2,1)} %all-gather.4.cloned.1.call-done, s32[1024]{0:T(1024)S(1)} %pad_clamp_fusion), kind=kCustom, calls=%fused_computation | custom fusion | bytes 25166080 | tf_op jit(solution)/shard_map/jit(_take)/gather | solution.py:38
  286.7 0.0 all-to-all-done
  286.7 22.1 %fusion.1 = f32[64,48,1024]{2,1,0:T(8,128)} fusion(bf16[64,1,48,2048]{3,2,1,0:T(8,128)(2,1)} %all-to-all-done, bf16[64,48,2048]{2,1,0:T(8,128)(2,1)} %gather_fusion, pred[64]{0:T(512)(128)(4,1)S(1)} %compare_and_fusion, bf16[1,2048,1024]{2,1,0:T(8,128)(2,1)} %param.9), kind=kOutput, calls=%fused_computation.3 | convolution fusion | flops 12916359168 | bytes 41943104 | tf_op jit(solution)/shard_map/dot_general | solution.py:40
  308.8 78.6 %all-gather.6.cloned.1.call-done = bf16[64,64,1024]{2,1,0:T(8,128)(2,1)} async-done(((bf16[1,64,1024]{2,1,0:T(8,128)(2,1)}), bf16[64,64,1024]{2,1,0:T(8,128)(2,1)}) %all-gather.6.cloned.1.call-update) | async-done | bytes 8388624 | tf_op jit(solution)/shard_map/all_gather | solution.py:45
  387.4 13.6 %fusion.12 = f32[64,1,48,64]{3,2,1,0:T(8,128)S(1)} fusion(bf16[64,64,1024]{2,1,0:T(8,128)(2,1)} %all-gather.6.cloned.1.call-done, f32[64,48,1024]{2,1,0:T(8,128)} %fusion.1, bf16[64,48,2048]{2,1,0:T(8,128)(2,1)} %gather_fusion, s32[]{:T(128)S(6)} %select_n.49, pred[64]{0:T(512)(128)(4,1)S(1)} %compare_and_fusion), kind=kOutput, calls=%fused_computation.15 | convolution fusion | flops 2425356288 | bytes 28049476 | tf_op jit(solution)/shard_map/kbp,kvp->kbv/dot_general | solution.py:46
  401.0 1.0 reshape.81
  401.9 21.3 %all_to_all.10 = f32[64,1,3072]{2,1,0:T(1,128)S(1)} all-to-all(f32[64,1,3072]{2,1,0:T(1,128)S(1)} %reshape.81), channel_id=1, replica_groups=mesh['ka'=64,'pa'=2] {'ka'}, dimensions={0} | all-to-all | bytes 1572864 | tf_op jit(solution)/shard_map/all_to_all | solution.py:14
  423.2 0.5 broadcast.61
  423.8 2.5 reduce.5
  426.3 0.4 reshape.82
  426.7 0.1 reduce_sum.33
  426.8 6.0 %all-gather = f32[96,64]{1,0:T(8,128)S(1)} all-gather(f32[48,64]{1,0:T(8,128)S(1)} %reduce_sum.33), channel_id=2, replica_groups=mesh['ka'=64,'pa'=2] {'pa'}, dimensions={0}, use_global_device_ids=true | all-gather | bytes 36864 | tf_op jit(solution)/shard_map/all_gather | solution.py:19
  432.8 0.6 reduce.4
  (5 shorter events, 0.0 us)
Async XLA Ops:
  6.5 268.2 %all-gather.4.cloned.1.call-start = ((), (), s32[]{:S(2)}) async-start(), calls=%async_computation.2 | async-start | bytes 12779520 | tf_op jit(solution)/shard_map/all_gather | solution.py:31
  14.2 11.1 %copy-start.1 = (s32[64]{0:T(128)S(1)}, s32[64]{0:T(128)}, u32[]{:S(2)}) copy-start(s32[64]{0:T(128)} %param.11) | copy-start | bytes 772
  14.2 11.7 %copy-start = (s32[64,64]{1,0:T(8,128)S(1)}, s32[64,64]{1,0:T(8,128)}, u32[]{:S(2)}) copy-start(s32[64,64]{1,0:T(8,128)} %param.10) | copy-start | bytes 49156
  14.2 272.5 %all-to-all-start = ((bf16[64,1,48,2048]{3,2,1,0:T(8,128)(2,1)}), bf16[64,1,48,2048]{3,2,1,0:T(8,128)(2,1)}, u32[]{:S(2)}, u32[]{:S(2)}) async-start(bf16[64,1,48,2048]{3,2,1,0:T(8,128)(2,1)} %stack.2), calls=%async_computation | async-start | bytes 25165824 | tf_op jit(solution)/shard_map/all_to_all | solution.py:33
  24.6 362.8 %all-gather.6.cloned.1.call-start = ((), (), s32[]{:S(2)}) async-start(), calls=%async_computation.3 | async-start | bytes 8519680 | tf_op jit(solution)/shard_map/all_gather | solution.py:45
Sparse Core Ops, SparseCore 0:
  9.0 265.6 all-gather.3
  276.5 110.8 all-gather.5
